TPU v7x, 256 devices: a whole 4x4x8 slice. The times are simulated.
256 devices in a mesh: rep: 4 (over y), fsdp: 64 (over x, z, core).
Axes of the slice: x: 4, y: 4, z: 8, core: 2. Of those that a mesh axis runs over, the one named last changes fastest.
Arguments:
- activations: bfloat16 [65536, 512], P(('rep', 'fsdp')), may hold values from -6 to 6
- output_grads: bfloat16 [65536, 8192], P(('rep', 'fsdp'))
- master: float32 [8192, 512], P('fsdp'), may hold values from -6 to 6
- first_moment: float32 [8192, 512], P('fsdp'), may hold values from -4 to 4
- second_moment: float32 [8192, 512], P('fsdp'), may hold values from 0.2 to 2
Outputs:
- new_master: float32 [8192, 512], P('fsdp')
- new_first: float32 [8192, 512], P('fsdp')
- new_second: float32 [8192, 512], P('fsdp')
- params: bfloat16 [8192, 512], replicated
All inputs are finite; a program needn't handle non-finite values.
Results may differ from a plain program's by a relative error of at most 0.0004.
Values may be sent and summed in bfloat16 or wider, within the bound.
No kernel may reach another device: no remote copies, remote signals or barrier semaphores. Data moves between devices by JAX's collectives and lax.ppermute only.
A program may use at most 128 MiB of HBM per device.

v0:
```python
import jax
import jax.numpy as jnp
from jax import lax
from jax.sharding import Mesh, PartitionSpec as P

dot_epsilon = 1e-06
beta_one = 0.9
beta_two = 0.95
adam_epsilon = 1e-08
learn_rate = 0.02
decay_rate = 0.1
contract_first = (((0,), (0,)), ((), ()))
GROUP = ("x", "z", "core")


def shifted(value, axis, step):
    size = lax.axis_size(axis)
    return lax.ppermute(value, axis, [(i, (i + step) % size) for i in range(size)])


def add_top(whole, part):
    rows = part.shape[0]
    return jnp.concatenate([whole[:rows] + part, whole[rows:]], axis=0)


def add_bottom(whole, part):
    rows = whole.shape[0] - part.shape[0]
    return jnp.concatenate([whole[:rows], whole[rows:] + part], axis=0)


def ring_reduce(chunk, axis):
    size = lax.axis_size(axis)
    half = size // 2
    far = chunk(half)
    rows = far.shape[0] // 2
    up = shifted(far[:rows], axis, 1)
    down = shifted(far[rows:], axis, -1)
    for reach in range(half - 1, 0, -1):
        if reach == half - 1:
            send_up, send_down = (add_top(chunk(reach), up), add_bottom(chunk(-reach), down))
        else:
            send_up, send_down = (chunk(reach) + up, chunk(-reach) + down)
        up = shifted(send_up, axis, 1)
        down = shifted(send_down, axis, -1)
    return chunk(0) + up + down


def by_place(whole, axis):
    size = lax.axis_size(axis)
    place = lax.axis_index(axis)

    def chunk(step):
        return lax.dynamic_index_in_dim(whole, (place + step + size) % size, 0, keepdims=False)

    return chunk


def group_members(own):
    place = lax.axis_index("rep")
    below, above, across = (shifted(own, "rep", 1), shifted(own, "rep", -1), shifted(own, "rep", 2))
    members = []
    for member in range(4):
        value = jnp.where(
            place == member,
            own,
            jnp.where(
                place == (member + 1) % 4,
                below,
                jnp.where(place == (member + 3) % 4, above, across),
            ),
        )
        members.append(value)
    return members


def pair_coefs(cross, left_sq, right_sq):
    return (
        1.0 - cross / (2.0 * (left_sq + dot_epsilon)),
        1.0 - cross / (2.0 * (right_sq + dot_epsilon)),
    )


def local(activations, output_grads, master, first_moment, second_moment):
    core = lax.axis_index("core")
    x_place = lax.axis_index("x")
    tokens, features = output_grads.shape
    width = activations.shape[1]
    rows = master.shape[0]
    half = width // 2
    with jax.named_scope("core_swap"):
        by_core = output_grads.reshape(tokens, features // (2 * rows), 2, rows)
        kept = jnp.where(core == 0, by_core[:, :, 0], by_core[:, :, 1]).reshape(
            tokens, features // 2
        )
        given = jnp.where(core == 0, by_core[:, :, 1], by_core[:, :, 0]).reshape(
            tokens, features // 2
        )
        grads = jnp.concatenate([kept, shifted(given, "core", 1)], axis=0)
        acts = jnp.concatenate([activations, shifted(activations, "core", 1)], axis=0)

    def product(grad_columns, act_columns):
        return lax.dot_general(
            grad_columns, act_columns, contract_first, preferred_element_type=jnp.float32
        )

    with jax.named_scope("reduce_b"):
        sums_b = product(grads, acts[:, half:]).reshape(4, 8, rows, half)
        sums_b = jnp.swapaxes(sums_b, 0, 1).reshape(8 * 4 * rows, half)
        sums_b = lax.psum_scatter(sums_b, "z", scatter_dimension=0, tiled=True)
    with jax.named_scope("reduce_a"):
        strip = features // 8

        def chunk_a(step):
            place = (x_place + step + 4) % 4
            return product(lax.dynamic_slice_in_dim(grads, place * strip, strip, 1), acts[:, :half])

        sums_a = ring_reduce(chunk_a, "x").reshape(8, rows, half)
        grad_a = ring_reduce(by_place(sums_a, "z"), "z")
    with jax.named_scope("reduce_b2"):
        grad_b = ring_reduce(by_place(sums_b.reshape(4, rows, half), "x"), "x")
    with jax.named_scope("members"):
        members_a = group_members(grad_a)
        members_b = group_members(grad_b)
        members = [jnp.concatenate(pair, axis=1) for pair in zip(members_a, members_b)]
    with jax.named_scope("gram"):
        pairs = [(i, j) for i in range(4) for j in range(i, 4)]
        sums = [jnp.sum(members[i] * members[j]) for i, j in pairs]
        row = jnp.concatenate([jnp.stack(sums), jnp.zeros((128 - len(sums),), jnp.float32)])
        everyone = lax.all_to_all(jnp.broadcast_to(row, (64, 1, 128)), GROUP, 0, 0)
        totals = jnp.sum(everyone, axis=(0, 1))
        gram = {pair: totals[index] for index, pair in enumerate(pairs)}
    with jax.named_scope("combine"):
        c0, c1 = pair_coefs(gram[0, 1], gram[0, 0], gram[1, 1])
        c2, c3 = pair_coefs(gram[2, 3], gram[2, 2], gram[3, 3])
        low_sq = c0 * c0 * gram[0, 0] + 2.0 * c0 * c1 * gram[0, 1] + c1 * c1 * gram[1, 1]
        high_sq = c2 * c2 * gram[2, 2] + 2.0 * c2 * c3 * gram[2, 3] + c3 * c3 * gram[3, 3]
        cross = c0 * (c2 * gram[0, 2] + c3 * gram[0, 3]) + c1 * (c2 * gram[1, 2] + c3 * gram[1, 3])
        low, high = pair_coefs(cross, jnp.maximum(low_sq, 0.0), jnp.maximum(high_sq, 0.0))
        combined = low * (c0 * members[0] + c1 * members[1]) + high * (
            c2 * members[2] + c3 * members[3]
        )
    with jax.named_scope("adamw"):
        correct_one = 1.0 - (beta_one**50) ** 2
        correct_two = 1.0 - (beta_two**50) ** 2
        new_first = beta_one * first_moment + (1.0 - beta_one) * combined
        new_second = beta_two * second_moment + (1.0 - beta_two) * combined * combined
        update = (
            new_first / correct_one / (jnp.sqrt(new_second / correct_two) + adam_epsilon)
            + decay_rate * master
        )
        new_master = master - learn_rate * update
    with jax.named_scope("params"):
        params = lax.all_gather(new_master.astype(jnp.bfloat16), GROUP, axis=0, tiled=True)
    return (new_master, new_first, new_second, params)


def solution(mesh):
    fine = Mesh(mesh.devices.reshape(4, 4, 8, 2), ("rep",) + GROUP)
    everyone = P(("rep",) + GROUP, None)
    block = P(GROUP, None)
    return jax.shard_map(
        local,
        mesh=fine,
        in_specs=(everyone, everyone, block, block, block),
        out_specs=(block, block, block, P()),
        check_vma=False,
    )
```

profile of v0, /device:TPU:1, one launch (start us, length us, event | category | flops | bytes accessed | tf_op | source)
XLA Modules:
  0.0 256.1 jit_solution(2416143929010002792)
XLA Ops:
  7.2 6.4 %copy.14 = bf16[256,8192]{0,1:T(8,128)(2,1)} copy(bf16[256,8192]{1,0:T(8,128)(2,1)} %param.6) | data formatting | bytes 8388608 | tf_op args[1]
  13.6 2.5 broadcast_select_fusion.1
  16.1 3.3 %collective-permute-start = (bf16[256,4096]{0,1:T(8,128)(2,1)S(1)}, bf16[256,4096]{0,1:T(8,128)(2,1)S(1)}, u32[]{:S(2)}, u32[]{:S(2)}) collective-permute-start(bf16[256,4096]{0,1:T(8,128)(2,1)S(1)} %bitcast.92), channel_id=1, source_target_pairs={{0,1},{1,0},{2,3},{3,2},{4,5},{5,4},{6,7},{7,6},{8,9},{9,8},{10,11... | collective-permute-start | bytes 6291464 | tf_op jit(solution)/shard_map/core_swap/ppermute | solution.py:18
  19.6 4.0 %collective-permute-done.1 = bf16[256,512]{1,0:T(8,128)(2,1)S(1)} collective-permute-done((bf16[256,512]{1,0:T(8,128)(2,1)S(1)}, bf16[256,512]{1,0:T(8,128)(2,1)S(1)}, u32[]{:S(2)}, u32[]{:S(2)}) %collective-permute-start.1) | collective-permute-done | bytes 262176 | tf_op jit(solution)/shard_map/core_swap/ppermute | solution.py:18
  25.0 2.3 copy.15
  33.3 10.0 %collective-permute-done.4 = f32[512,256]{1,0:T(8,128)S(1)} collective-permute-done((f32[512,256]{1,0:T(8,128)}, f32[512,256]{1,0:T(8,128)S(1)}, u32[]{:S(2)}, u32[]{:S(2)}) %collective-permute-start.4) | collective-permute-done | bytes 524320 | tf_op jit(solution)/shard_map/reduce_a/ppermute | solution.py:18
  43.6 1.9 collective-permute-start.5
  46.6 20.6 %collective-permute-done.5 = f32[1024,256]{1,0:T(8,128)} collective-permute-done((f32[1024,256]{1,0:T(8,128)S(1)}, f32[1024,256]{1,0:T(8,128)}, u32[]{:S(2)}, u32[]{:S(2)}) %collective-permute-start.5) | collective-permute-done | bytes 1048608 | tf_op jit(solution)/shard_map/reduce_a/ppermute | solution.py:18
  67.3 4.0 %collective-permute-done.3 = f32[1024,256]{1,0:T(8,128)} collective-permute-done((f32[1024,256]{1,0:T(8,128)}, f32[1024,256]{1,0:T(8,128)}, u32[]{:S(2)}, u32[]{:S(2)}) %collective-permute-start.3) | collective-permute-done | bytes 1048608 | tf_op jit(solution)/shard_map/reduce_a/ppermute | solution.py:18
  71.3 2.2 fusion.1
  75.3 4.3 %collective-permute-start.10 = (f32[64,256]{1,0:T(8,128)S(1)}, f32[64,256]{1,0:T(8,128)S(1)}, u32[]{:S(2)}, u32[]{:S(2)}) collective-permute-start(f32[64,256]{1,0:T(8,128)S(1)} %get-tuple-element.26), channel_id=1, source_target_pairs={{0,14},{2,0},{4,2},{6,4},{8,6},{10,8},{12,10},{14,12},{1,15},{3,1}... | collective-permute-start | bytes 196616 | tf_op jit(solution)/shard_map/reduce_a/ppermute | solution.py:18
  79.6 3.5 %collective-permute-done.6 = f32[64,256]{1,0:T(8,128)S(1)} collective-permute-done((f32[64,256]{1,0:T(8,128)S(1)}, f32[64,256]{1,0:T(8,128)S(1)}, u32[]{:S(2)}, u32[]{:S(2)}) %collective-permute-start.6) | collective-permute-done | bytes 65568 | tf_op jit(solution)/shard_map/reduce_a/ppermute | solution.py:18
  83.3 2.7 %collective-permute-start.11 = (f32[128,256]{1,0:T(8,128)S(1)}, f32[128,256]{1,0:T(8,128)S(1)}, u32[]{:S(2)}, u32[]{:S(2)}) collective-permute-start(f32[128,256]{1,0:T(8,128)S(1)} %pad_maximum_fusion.9), channel_id=1, source_target_pairs={{0,14},{2,0},{4,2},{6,4},{8,6},{10,8},{12,10},{14,12},{1,15},{3,1}... | collective-permute-start | bytes 393224 | tf_op jit(solution)/shard_map/reduce_a/ppermute | solution.py:18
  86.0 2.3 collective-permute-done.7
  88.6 5.0 %collective-permute-done.8 = f32[128,256]{1,0:T(8,128)S(1)} collective-permute-done((f32[128,256]{1,0:T(8,128)S(1)}, f32[128,256]{1,0:T(8,128)S(1)}, u32[]{:S(2)}, u32[]{:S(2)}) %collective-permute-start.8) | collective-permute-done | bytes 131104 | tf_op jit(solution)/shard_map/reduce_a/ppermute | solution.py:18
  96.2 2.7 %collective-permute-start.19 = (f32[64,256]{1,0:T(8,128)S(1)}, f32[64,256]{1,0:T(8,128)S(1)}, u32[]{:S(2)}, u32[]{:S(2)}) collective-permute-start(f32[64,256]{1,0:T(8,128)S(1)} %get-tuple-element.50), channel_id=1, source_target_pairs={{0,48},{16,0},{32,16},{48,32},{1,49},{17,1},{33,17},{49,33},{2,50}... | collective-permute-start | bytes 196616 | tf_op jit(solution)/shard_map/reduce_b2/ppermute | solution.py:18
  101.4 3.0 %collective-permute-start.20 = (f32[128,256]{1,0:T(8,128)S(1)}, f32[128,256]{1,0:T(8,128)S(1)}, u32[]{:S(2)}, u32[]{:S(2)}) collective-permute-start(f32[128,256]{1,0:T(8,128)S(1)} %pad_maximum_fusion.11), channel_id=1, source_target_pairs={{0,48},{16,0},{32,16},{48,32},{1,49},{17,1},{33,17},{49,33},{2,50}... | collective-permute-start | bytes 393224 | tf_op jit(solution)/shard_map/reduce_b2/ppermute | solution.py:18
  104.7 3.0 %collective-permute-start.16 = (f32[128,256]{1,0:T(8,128)S(1)}, f32[128,256]{1,0:T(8,128)S(1)}, u32[]{:S(2)}, u32[]{:S(2)}) collective-permute-start(f32[128,256]{1,0:T(8,128)S(1)} %fusion.20), channel_id=1, source_target_pairs={{0,128},{64,192},{128,0},{192,64},{1,129},{65,193},{129,1},{193,65... | collective-permute-start | bytes 393224 | tf_op jit(solution)/shard_map/members/ppermute | solution.py:18
  110.5 3.0 %collective-permute-start.23 = (f32[128,256]{1,0:T(8,128)S(1)}, f32[128,256]{1,0:T(8,128)S(1)}, u32[]{:S(2)}, u32[]{:S(2)}) collective-permute-start(f32[128,256]{1,0:T(8,128)S(1)} %fusion.19), channel_id=1, source_target_pairs={{0,128},{64,192},{128,0},{192,64},{1,129},{65,193},{129,1},{193,65... | collective-permute-start | bytes 393224 | tf_op jit(solution)/shard_map/members/ppermute | solution.py:18
  116.7 2.5 collective-permute-done.22
  120.3 6.4 %concatenate.51 = f32[128]{0:T(128)S(1)} concatenate(f32[1]{0:T(128)} %bitcast.26, f32[1]{0:T(128)} %bitcast.27, f32[1]{0:T(128)} %bitcast.28, f32[1]{0:T(128)} %bitcast.29, f32[1]{0:T(128)} %bitcast.30, f32[1]{0:T(128)} %bitcast.31, f32[1]{0:T(128)} %bitcast.32, f32[1]{0:T(128)} %bitcast.33, f32[1]{0:T(128)} %bitcast.34, f32[1]{0:T(128)} %bitcast.35, f32[118]{0:T(128)S(1)} %broadcast_in_dim.6), dimensions={0} | concatenate | bytes 1024 | tf_op jit(solution)/shard_map/gram/concatenate | solution.py:128
  126.8 25.9 %all_to_all.5 = f32[64,1,128]{2,1,0:T(1,128)S(1)} all-to-all(f32[64,1,128]{2,1,0:T(1,128)S(1)} %broadcast_in_dim.7), channel_id=1, replica_groups=mesh['rep'=4,'x'=4,'z'=8,'core'=2] {'x','z','core'}, dimensions={0} | all-to-all | bytes 65536 | tf_op jit(solution)/shard_map/gram/all_to_all | solution.py:129
  166.0 75.9 %all-gather.2.cloned.1.call-done = bf16[8192,512]{1,0:T(8,128)(2,1)} async-done(((bf16[128,512]{1,0:T(8,128)(2,1)}), bf16[8192,512]{1,0:T(8,128)(2,1)}) %all-gather.2.cloned.1.call-update) | async-done | bytes 8388624 | tf_op jit(solution)/shard_map/params/all_gather | solution.py:153
  241.9 7.3 %copy.19 = bf16[8192,512]{1,0:T(8,128)(2,1)} copy(bf16[8192,512]{1,0:T(8,128)(2,1)} %all-gather.2.cloned.1.call-done) | data formatting | bytes 16777216
  (83 shorter events, 25.2 us)
Async XLA Ops:
  7.2 88.0 %reduce-scatter.2.cloned.1.call-start = ((), (), s32[]{:S(2)}) async-start(), calls=%async_computation.2 | async-start | bytes 4718592 | tf_op jit(solution)/shard_map/reduce_b/reduce_scatter | solution.py:109
  16.1 7.5 %collective-permute-start = (bf16[256,4096]{0,1:T(8,128)(2,1)S(1)}, bf16[256,4096]{0,1:T(8,128)(2,1)S(1)}, u32[]{:S(2)}, u32[]{:S(2)}) collective-permute-start(bf16[256,4096]{0,1:T(8,128)(2,1)S(1)} %bitcast.92), channel_id=1, source_target_pairs={{0,1},{1,0},{2,3},{3,2},{4,5},{5,4},{6,7},{7,6},{8,9},{9,8},{10,11... | collective-permute-start | bytes 6291464 | tf_op jit(solution)/shard_map/core_swap/ppermute | solution.py:18
  27.3 214.6 %all-gather.2.cloned.1.call-start = ((), (), s32[]{:S(2)}) async-start(), calls=%async_computation.3 | async-start | bytes 8519680 | tf_op jit(solution)/shard_map/params/all_gather | solution.py:153
  29.9 13.4 %collective-permute-start.4 = (f32[512,256]{1,0:T(8,128)}, f32[512,256]{1,0:T(8,128)S(1)}, u32[]{:S(2)}, u32[]{:S(2)}) collective-permute-start(f32[512,256]{1,0:T(8,128)} %get-tuple-element.31), channel_id=1, source_target_pairs={{0,48},{16,0},{32,16},{48,32},{1,49},{17,1},{33,17},{49,33},{2,50}... | collective-permute-start | bytes 1572872 | tf_op jit(solution)/shard_map/reduce_a/ppermute | solution.py:18
  30.7 14.8 %collective-permute-start.2 = (f32[512,256]{1,0:T(8,128)}, f32[512,256]{1,0:T(8,128)S(1)}, u32[]{:S(2)}, u32[]{:S(2)}) collective-permute-start(f32[512,256]{1,0:T(8,128)} %get-tuple-element.30), channel_id=1, source_target_pairs={{0,16},{16,32},{32,48},{48,0},{1,17},{17,33},{33,49},{49,1},{2,18}... | collective-permute-start | bytes 1572872 | tf_op jit(solution)/shard_map/reduce_a/ppermute | solution.py:18
  43.6 23.7 %collective-permute-start.5 = (f32[1024,256]{1,0:T(8,128)S(1)}, f32[1024,256]{1,0:T(8,128)}, u32[]{:S(2)}, u32[]{:S(2)}) collective-permute-start(f32[1024,256]{1,0:T(8,128)S(1)} %pad_maximum_fusion.3), channel_id=1, source_target_pairs={{0,48},{16,0},{32,16},{48,32},{1,49},{17,1},{33,17},{49,33},{2,50}... | collective-permute-start | bytes 3145736 | tf_op jit(solution)/shard_map/reduce_a/ppermute | solution.py:18
  46.6 24.7 %collective-permute-start.3 = (f32[1024,256]{1,0:T(8,128)}, f32[1024,256]{1,0:T(8,128)}, u32[]{:S(2)}, u32[]{:S(2)}) collective-permute-start(f32[1024,256]{1,0:T(8,128)} %pad_maximum_fusion.2), channel_id=1, source_target_pairs={{0,16},{16,32},{32,48},{48,0},{1,17},{17,33},{33,49},{49,1},{2,18}... | collective-permute-start | bytes 3145736 | tf_op jit(solution)/shard_map/reduce_a/ppermute | solution.py:18
  73.6 9.5 %collective-permute-start.6 = (f32[64,256]{1,0:T(8,128)S(1)}, f32[64,256]{1,0:T(8,128)S(1)}, u32[]{:S(2)}, u32[]{:S(2)}) collective-permute-start(f32[64,256]{1,0:T(8,128)S(1)} %get-tuple-element.24), channel_id=1, source_target_pairs={{0,2},{2,4},{4,6},{6,8},{8,10},{10,12},{12,14},{14,0},{1,3},{3,5},... | collective-permute-start | bytes 196616 | tf_op jit(solution)/shard_map/reduce_a/ppermute | solution.py:18
  75.3 7.8 %collective-permute-start.10 = (f32[64,256]{1,0:T(8,128)S(1)}, f32[64,256]{1,0:T(8,128)S(1)}, u32[]{:S(2)}, u32[]{:S(2)}) collective-permute-start(f32[64,256]{1,0:T(8,128)S(1)} %get-tuple-element.26), channel_id=1, source_target_pairs={{0,14},{2,0},{4,2},{6,4},{8,6},{10,8},{12,10},{14,12},{1,15},{3,1}... | collective-permute-start | bytes 196616 | tf_op jit(solution)/shard_map/reduce_a/ppermute | solution.py:18
  83.2 5.1 %collective-permute-start.7 = (f32[128,256]{1,0:T(8,128)S(1)}, f32[128,256]{1,0:T(8,128)S(1)}, u32[]{:S(2)}, u32[]{:S(2)}) collective-permute-start(f32[128,256]{1,0:T(8,128)S(1)} %pad_maximum_fusion.8), channel_id=1, source_target_pairs={{0,2},{2,4},{4,6},{6,8},{8,10},{10,12},{12,14},{14,0},{1,3},{3,5},... | collective-permute-start | bytes 393224 | tf_op jit(solution)/shard_map/reduce_a/ppermute | solution.py:18
  83.3 5.3 %collective-permute-start.11 = (f32[128,256]{1,0:T(8,128)S(1)}, f32[128,256]{1,0:T(8,128)S(1)}, u32[]{:S(2)}, u32[]{:S(2)}) collective-permute-start(f32[128,256]{1,0:T(8,128)S(1)} %pad_maximum_fusion.9), channel_id=1, source_target_pairs={{0,14},{2,0},{4,2},{6,4},{8,6},{10,8},{12,10},{14,12},{1,15},{3,1}... | collective-permute-start | bytes 393224 | tf_op jit(solution)/shard_map/reduce_a/ppermute | solution.py:18
  88.3 5.3 %collective-permute-start.8 = (f32[128,256]{1,0:T(8,128)S(1)}, f32[128,256]{1,0:T(8,128)S(1)}, u32[]{:S(2)}, u32[]{:S(2)}) collective-permute-start(f32[128,256]{1,0:T(8,128)S(1)} %bitcast_add_fusion.3), channel_id=1, source_target_pairs={{0,2},{2,4},{4,6},{6,8},{8,10},{10,12},{12,14},{14,0},{1,3},{3,5},... | collective-permute-start | bytes 393224 | tf_op jit(solution)/shard_map/reduce_a/ppermute | solution.py:18
  93.6 5.3 %collective-permute-start.12 = (f32[128,256]{1,0:T(8,128)S(1)}, f32[128,256]{1,0:T(8,128)S(1)}, u32[]{:S(2)}, u32[]{:S(2)}) collective-permute-start(f32[128,256]{1,0:T(8,128)S(1)} %get-tuple-element.21), channel_id=1, source_target_pairs={{0,14},{2,0},{4,2},{6,4},{8,6},{10,8},{12,10},{14,12},{1,15},{3,1}... | collective-permute-start | bytes 393224 | tf_op jit(solution)/shard_map/reduce_a/ppermute | solution.py:18
  93.8 10.8 %collective-permute-start.9 = (f32[128,256]{1,0:T(8,128)S(1)}, f32[128,256]{1,0:T(8,128)S(1)}, u32[]{:S(2)}, u32[]{:S(2)}) collective-permute-start(f32[128,256]{1,0:T(8,128)S(1)} %get-tuple-element.20), channel_id=1, source_target_pairs={{0,2},{2,4},{4,6},{6,8},{8,10},{10,12},{12,14},{14,0},{1,3},{3,5},... | collective-permute-start | bytes 393224 | tf_op jit(solution)/shard_map/reduce_a/ppermute | solution.py:18
  96.1 4.4 %collective-permute-start.17 = (f32[64,256]{1,0:T(8,128)S(1)}, f32[64,256]{1,0:T(8,128)S(1)}, u32[]{:S(2)}, u32[]{:S(2)}) collective-permute-start(f32[64,256]{1,0:T(8,128)S(1)} %get-tuple-element.48), channel_id=1, source_target_pairs={{0,16},{16,32},{32,48},{48,0},{1,17},{17,33},{33,49},{49,1},{2,18}... | collective-permute-start | bytes 196616 | tf_op jit(solution)/shard_map/reduce_b2/ppermute | solution.py:18
  98.9 5.7 %collective-permute-start.13 = (f32[128,256]{1,0:T(8,128)S(1)}, f32[128,256]{1,0:T(8,128)S(1)}, u32[]{:S(2)}, u32[]{:S(2)}) collective-permute-start(f32[128,256]{1,0:T(8,128)S(1)} %bitcast_add_fusion.2), channel_id=1, source_target_pairs={{0,14},{2,0},{4,2},{6,4},{8,6},{10,8},{12,10},{14,12},{1,15},{3,1}... | collective-permute-start | bytes 393224 | tf_op jit(solution)/shard_map/reduce_a/ppermute | solution.py:18
  101.4 7.7 %collective-permute-start.20 = (f32[128,256]{1,0:T(8,128)S(1)}, f32[128,256]{1,0:T(8,128)S(1)}, u32[]{:S(2)}, u32[]{:S(2)}) collective-permute-start(f32[128,256]{1,0:T(8,128)S(1)} %pad_maximum_fusion.11), channel_id=1, source_target_pairs={{0,48},{16,0},{32,16},{48,32},{1,49},{17,1},{33,17},{49,33},{2,50}... | collective-permute-start | bytes 393224 | tf_op jit(solution)/shard_map/reduce_b2/ppermute | solution.py:18
  104.5 5.1 %collective-permute-start.18 = (f32[128,256]{1,0:T(8,128)S(1)}, f32[128,256]{1,0:T(8,128)S(1)}, u32[]{:S(2)}, u32[]{:S(2)}) collective-permute-start(f32[128,256]{1,0:T(8,128)S(1)} %pad_maximum_fusion.10), channel_id=1, source_target_pairs={{0,16},{16,32},{32,48},{48,0},{1,17},{17,33},{33,49},{49,1},{2,18}... | collective-permute-start | bytes 393224 | tf_op jit(solution)/shard_map/reduce_b2/ppermute | solution.py:18
  104.7 9.6 %collective-permute-start.16 = (f32[128,256]{1,0:T(8,128)S(1)}, f32[128,256]{1,0:T(8,128)S(1)}, u32[]{:S(2)}, u32[]{:S(2)}) collective-permute-start(f32[128,256]{1,0:T(8,128)S(1)} %fusion.20), channel_id=1, source_target_pairs={{0,128},{64,192},{128,0},{192,64},{1,129},{65,193},{129,1},{193,65... | collective-permute-start | bytes 393224 | tf_op jit(solution)/shard_map/members/ppermute | solution.py:18
  107.7 7.3 %collective-permute-start.15 = (f32[128,256]{1,0:T(8,128)S(1)}, f32[128,256]{1,0:T(8,128)S(1)}, u32[]{:S(2)}, u32[]{:S(2)}) collective-permute-start(f32[128,256]{1,0:T(8,128)S(1)} %fusion.20), channel_id=1, source_target_pairs={{0,192},{64,0},{128,64},{192,128},{1,193},{65,1},{129,65},{193,129... | collective-permute-start | bytes 393224 | tf_op jit(solution)/shard_map/members/ppermute | solution.py:18
  108.5 6.5 %collective-permute-start.14 = (f32[128,256]{1,0:T(8,128)S(1)}, f32[128,256]{1,0:T(8,128)S(1)}, u32[]{:S(2)}, u32[]{:S(2)}) collective-permute-start(f32[128,256]{1,0:T(8,128)S(1)} %fusion.20), channel_id=1, source_target_pairs={{0,64},{64,128},{128,192},{192,0},{1,65},{65,129},{129,193},{193,1... | collective-permute-start | bytes 393224 | tf_op jit(solution)/shard_map/members/ppermute | solution.py:18
  110.5 6.2 %collective-permute-start.23 = (f32[128,256]{1,0:T(8,128)S(1)}, f32[128,256]{1,0:T(8,128)S(1)}, u32[]{:S(2)}, u32[]{:S(2)}) collective-permute-start(f32[128,256]{1,0:T(8,128)S(1)} %fusion.19), channel_id=1, source_target_pairs={{0,128},{64,192},{128,0},{192,64},{1,129},{65,193},{129,1},{193,65... | collective-permute-start | bytes 393224 | tf_op jit(solution)/shard_map/members/ppermute | solution.py:18
  113.5 5.6 %collective-permute-start.22 = (f32[128,256]{1,0:T(8,128)S(1)}, f32[128,256]{1,0:T(8,128)S(1)}, u32[]{:S(2)}, u32[]{:S(2)}) collective-permute-start(f32[128,256]{1,0:T(8,128)S(1)} %fusion.19), channel_id=1, source_target_pairs={{0,192},{64,0},{128,64},{192,128},{1,193},{65,1},{129,65},{193,129... | collective-permute-start | bytes 393224 | tf_op jit(solution)/shard_map/members/ppermute | solution.py:18
  114.3 5.1 %collective-permute-start.21 = (f32[128,256]{1,0:T(8,128)S(1)}, f32[128,256]{1,0:T(8,128)S(1)}, u32[]{:S(2)}, u32[]{:S(2)}) collective-permute-start(f32[128,256]{1,0:T(8,128)S(1)} %fusion.19), channel_id=1, source_target_pairs={{0,64},{64,128},{128,192},{192,0},{1,65},{65,129},{129,193},{193,1... | collective-permute-start | bytes 393224 | tf_op jit(solution)/shard_map/members/ppermute | solution.py:18
  (9 other events, 207.8 us)
Sparse Core Ops, SparseCore 0:
  27.5 56.9 reduce-scatter.1
  166.2 75.7 all-gather.1
where the time goes:
time: 257 us; the launch traced here: 256 us
  waiting for transfers between devices  130 us (51%)
  starting transfers between devices  33.6 us (13%)
  between operations  26 us (10%)
  blocking collectives  25.9 us (10%)
  local copies, waits for them, and re-layouts  25.2 us (10%)
  other arithmetic  7.97 us (3%)
  matrix products  6.9 us (3%)
    all_gather x1, waiting for transfers between devices, local(): lax.all_gather(new_master.astype(jnp.bfloat16), GROUP, axis=0, tiled=True)  75.9 us
    ppermute x24, waiting for transfers between devices, shifted(): lax.ppermute(value, axis, [(i, (i + step) % size) for i in range(size)])  54.5 us
    ppermute x24, starting transfers between devices, shifted(): lax.ppermute(value, axis, [(i, (i + step) % size) for i in range(size)])  33.6 us
    all_to_all x1, blocking collectives, local(): everyone = lax.all_to_all(jnp.broadcast_to(row, (64, 1, 128)), GROUP, 0, 0)  25.9 us
    unnamed x17, local copies, waits for them, and re-layouts  13.8 us
    dot_general x5, matrix products, product(): lax.dot_general(grad_columns, act_columns, contract_first, preferred_elem...  6.9 us
    concatenate x1, local copies, waits for them, and re-layouts, local(): jnp.concatenate([jnp.stack(sums), jnp.zeros((128 - len(sums),), jnp.float...  6.4 us
  transfers between devices with their start and end apart: 26, of which 13 were waited for; matrix products, arithmetic and copies ran while one was open for 4% of the time, Pallas kernels for 0%

commit v1 on v0

--- a/solution.py
+++ b/solution.py
@@ -150,7 +150,12 @@
         )
         new_master = master - learn_rate * update
     with jax.named_scope("params"):
-        params = lax.all_gather(new_master.astype(jnp.bfloat16), GROUP, axis=0, tiled=True)
+        params = jnp.concatenate(
+            lax.all_to_all(
+                jnp.stack([new_master.astype(jnp.bfloat16)] * lax.axis_size(GROUP)), GROUP, 0, 0
+            ),
+            axis=0,
+        )
     return (new_master, new_first, new_second, params)
 
 

time: 257 us -> 372 us (1.45)
  blocking collectives: 25.9 us -> 217 us
  waiting for transfers between devices: 130 us -> 54.5 us
    all_to_all x0 -> x1, blocking collectives: none -> 191 us  [local(): lax.all_to_all(jnp.stack([new_master.astype(jnp.bfloat16)] * lax.axis_siz...]
    all_gather x1 -> x0, waiting for transfers between devices: 75.9 us -> none  [local(): lax.all_gather(new_master.astype(jnp.bfloat16), GROUP, axis=0, tiled=True)]
  transfers between devices with their start and end apart: 26 -> 25, of which waited for: 13 -> 11; matrix products, arithmetic and copies ran while one was open for 4% -> 3% of each run, Pallas kernels for 0% -> 0%
where the time goes in v1:
time: 372 us
  blocking collectives  217 us (58%)
  waiting for transfers between devices  54.5 us (15%)
  starting transfers between devices  33.6 us (9%)
  local copies, waits for them, and re-layouts  26.1 us (7%)
  between operations  25.7 us (7%)
  other arithmetic  7.89 us (2%)
  matrix products  6.9 us (2%)
    all_to_all x1, blocking collectives, local(): lax.all_to_all(jnp.stack([new_master.astype(jnp.bfloat16)] * lax.axis_siz...  191 us
    ppermute x24, waiting for transfers between devices, shifted(): lax.ppermute(value, axis, [(i, (i + step) % size) for i in range(size)])  54.5 us
    ppermute x24, starting transfers between devices, shifted(): lax.ppermute(value, axis, [(i, (i + step) % size) for i in range(size)])  33.6 us
    all_to_all x1, blocking collectives, local(): everyone = lax.all_to_all(jnp.broadcast_to(row, (64, 1, 128)), GROUP, 0, 0)  25.9 us
    unnamed x17, local copies, waits for them, and re-layouts  13.8 us
  transfers between devices with their start and end apart: 25, of which 11 were waited for; matrix products, arithmetic and copies ran while one was open for 3% of the time, Pallas kernels for 0%

profile of v1, /device:TPU:1, one launch (start us, length us, event | category | flops | bytes accessed | tf_op | source)
XLA Modules:
  0.0 371.6 jit_solution(11007948250555621606)
XLA Ops:
  7.2 6.4 %copy.14 = bf16[256,8192]{0,1:T(8,128)(2,1)} copy(bf16[256,8192]{1,0:T(8,128)(2,1)} %param.6) | data formatting | bytes 8388608 | tf_op args[1]
  13.6 2.5 broadcast_select_fusion.1
  16.1 3.3 collective-permute-start
  19.6 4.0 %collective-permute-done.1 = bf16[256,512]{1,0:T(8,128)(2,1)S(1)} collective-permute-done((bf16[256,512]{1,0:T(8,128)(2,1)S(1)}, bf16[256,512]{1,0:T(8,128)(2,1)S(1)}, u32[]{:S(2)}, u32[]{:S(2)}) %collective-permute-start.1) | collective-permute-done | bytes 262176 | tf_op jit(solution)/shard_map/core_swap/ppermute | solution.py:18
  25.0 2.3 copy.15
  33.3 10.0 %collective-permute-done.4 = f32[512,256]{1,0:T(8,128)S(1)} collective-permute-done((f32[512,256]{1,0:T(8,128)}, f32[512,256]{1,0:T(8,128)S(1)}, u32[]{:S(2)}, u32[]{:S(2)}) %collective-permute-start.4) | collective-permute-done | bytes 524320 | tf_op jit(solution)/shard_map/reduce_a/ppermute | solution.py:18
  43.5 1.9 collective-permute-start.5
  46.6 20.7 %collective-permute-done.5 = f32[1024,256]{1,0:T(8,128)} collective-permute-done((f32[1024,256]{1,0:T(8,128)S(1)}, f32[1024,256]{1,0:T(8,128)}, u32[]{:S(2)}, u32[]{:S(2)}) %collective-permute-start.5) | collective-permute-done | bytes 1048608 | tf_op jit(solution)/shard_map/reduce_a/ppermute | solution.py:18
  67.3 4.0 %collective-permute-done.3 = f32[1024,256]{1,0:T(8,128)} collective-permute-done((f32[1024,256]{1,0:T(8,128)}, f32[1024,256]{1,0:T(8,128)}, u32[]{:S(2)}, u32[]{:S(2)}) %collective-permute-start.3) | collective-permute-done | bytes 1048608 | tf_op jit(solution)/shard_map/reduce_a/ppermute | solution.py:18
  71.3 2.2 fusion.1
  75.3 4.3 %collective-permute-start.10 = (f32[64,256]{1,0:T(8,128)S(1)}, f32[64,256]{1,0:T(8,128)S(1)}, u32[]{:S(2)}, u32[]{:S(2)}) collective-permute-start(f32[64,256]{1,0:T(8,128)S(1)} %get-tuple-element.26), channel_id=1, source_target_pairs={{0,14},{2,0},{4,2},{6,4},{8,6},{10,8},{12,10},{14,12},{1,15},{3,1}... | collective-permute-start | bytes 196616 | tf_op jit(solution)/shard_map/reduce_a/ppermute | solution.py:18
  79.6 3.5 collective-permute-done.6
  83.3 2.7 collective-permute-start.11
  86.0 2.3 collective-permute-done.7
  88.6 5.0 %collective-permute-done.8 = f32[128,256]{1,0:T(8,128)S(1)} collective-permute-done((f32[128,256]{1,0:T(8,128)S(1)}, f32[128,256]{1,0:T(8,128)S(1)}, u32[]{:S(2)}, u32[]{:S(2)}) %collective-permute-start.8) | collective-permute-done | bytes 131104 | tf_op jit(solution)/shard_map/reduce_a/ppermute | solution.py:18
  96.2 2.7 collective-permute-start.19
  101.4 3.0 collective-permute-start.20
  104.7 3.0 collective-permute-start.16
  110.5 3.0 collective-permute-start.23
  116.8 2.6 collective-permute-done.22
  120.3 6.3 %concatenate.51 = f32[128]{0:T(128)S(1)} concatenate(f32[1]{0:T(128)} %bitcast.26, f32[1]{0:T(128)} %bitcast.27, f32[1]{0:T(128)} %bitcast.28, f32[1]{0:T(128)} %bitcast.29, f32[1]{0:T(128)} %bitcast.30, f32[1]{0:T(128)} %bitcast.31, f32[1]{0:T(128)} %bitcast.32, f32[1]{0:T(128)} %bitcast.33, f32[1]{0:T(128)} %bitcast.34, f32[1]{0:T(128)} %bitcast.35, f32[118]{0:T(128)S(1)} %broadcast_in_dim.6), dimensions={0} | concatenate | bytes 1024 | tf_op jit(solution)/shard_map/gram/concatenate | solution.py:128
  126.6 25.9 %all_to_all.10 = f32[64,1,128]{2,1,0:T(1,128)S(1)} all-to-all(f32[64,1,128]{2,1,0:T(1,128)S(1)} %broadcast_in_dim.7), channel_id=1, replica_groups=mesh['rep'=4,'x'=4,'z'=8,'core'=2] {'x','z','core'}, dimensions={0} | all-to-all | bytes 65536 | tf_op jit(solution)/shard_map/gram/all_to_all | solution.py:129
  166.6 190.8 %all_to_all.11 = bf16[64,128,512]{2,1,0:T(8,128)(2,1)} all-to-all(bf16[64,128,512]{2,1,0:T(8,128)(2,1)S(1)} %stack.32), channel_id=1, replica_groups=mesh['rep'=4,'x'=4,'z'=8,'core'=2] {'x','z','core'}, dimensions={0} | all-to-all | bytes 16777216 | tf_op jit(solution)/shard_map/params/all_to_all | solution.py:154
  357.4 7.3 %copy.19 = bf16[8192,512]{1,0:T(8,128)(2,1)} copy(bf16[8192,512]{1,0:T(8,128)(2,1)} %bitcast.84) | data formatting | bytes 16777216
  (82 shorter events, 26.0 us)
Async XLA Ops:
  7.2 88.0 %reduce-scatter.2.cloned.1.call-start = ((), (), s32[]{:S(2)}) async-start(), calls=%async_computation.3 | async-start | bytes 4718592 | tf_op jit(solution)/shard_map/reduce_b/reduce_scatter | solution.py:109
  16.1 7.5 %collective-permute-start = (bf16[256,4096]{0,1:T(8,128)(2,1)S(1)}, bf16[256,4096]{0,1:T(8,128)(2,1)S(1)}, u32[]{:S(2)}, u32[]{:S(2)}) collective-permute-start(bf16[256,4096]{0,1:T(8,128)(2,1)S(1)} %bitcast.94), channel_id=1, source_target_pairs={{0,1},{1,0},{2,3},{3,2},{4,5},{5,4},{6,7},{7,6},{8,9},{9,8},{10,11... | collective-permute-start | bytes 6291464 | tf_op jit(solution)/shard_map/core_swap/ppermute | solution.py:18
  29.9 13.4 %collective-permute-start.4 = (f32[512,256]{1,0:T(8,128)}, f32[512,256]{1,0:T(8,128)S(1)}, u32[]{:S(2)}, u32[]{:S(2)}) collective-permute-start(f32[512,256]{1,0:T(8,128)} %get-tuple-element.31), channel_id=1, source_target_pairs={{0,48},{16,0},{32,16},{48,32},{1,49},{17,1},{33,17},{49,33},{2,50}... | collective-permute-start | bytes 1572872 | tf_op jit(solution)/shard_map/reduce_a/ppermute | solution.py:18
  30.6 14.8 %collective-permute-start.2 = (f32[512,256]{1,0:T(8,128)}, f32[512,256]{1,0:T(8,128)S(1)}, u32[]{:S(2)}, u32[]{:S(2)}) collective-permute-start(f32[512,256]{1,0:T(8,128)} %get-tuple-element.30), channel_id=1, source_target_pairs={{0,16},{16,32},{32,48},{48,0},{1,17},{17,33},{33,49},{49,1},{2,18}... | collective-permute-start | bytes 1572872 | tf_op jit(solution)/shard_map/reduce_a/ppermute | solution.py:18
  43.5 23.7 %collective-permute-start.5 = (f32[1024,256]{1,0:T(8,128)S(1)}, f32[1024,256]{1,0:T(8,128)}, u32[]{:S(2)}, u32[]{:S(2)}) collective-permute-start(f32[1024,256]{1,0:T(8,128)S(1)} %pad_maximum_fusion.3), channel_id=1, source_target_pairs={{0,48},{16,0},{32,16},{48,32},{1,49},{17,1},{33,17},{49,33},{2,50}... | collective-permute-start | bytes 3145736 | tf_op jit(solution)/shard_map/reduce_a/ppermute | solution.py:18
  46.6 24.7 %collective-permute-start.3 = (f32[1024,256]{1,0:T(8,128)}, f32[1024,256]{1,0:T(8,128)}, u32[]{:S(2)}, u32[]{:S(2)}) collective-permute-start(f32[1024,256]{1,0:T(8,128)} %pad_maximum_fusion.2), channel_id=1, source_target_pairs={{0,16},{16,32},{32,48},{48,0},{1,17},{17,33},{33,49},{49,1},{2,18}... | collective-permute-start | bytes 3145736 | tf_op jit(solution)/shard_map/reduce_a/ppermute | solution.py:18
  73.6 9.5 %collective-permute-start.6 = (f32[64,256]{1,0:T(8,128)S(1)}, f32[64,256]{1,0:T(8,128)S(1)}, u32[]{:S(2)}, u32[]{:S(2)}) collective-permute-start(f32[64,256]{1,0:T(8,128)S(1)} %get-tuple-element.24), channel_id=1, source_target_pairs={{0,2},{2,4},{4,6},{6,8},{8,10},{10,12},{12,14},{14,0},{1,3},{3,5},... | collective-permute-start | bytes 196616 | tf_op jit(solution)/shard_map/reduce_a/ppermute | solution.py:18
  75.3 7.8 %collective-permute-start.10 = (f32[64,256]{1,0:T(8,128)S(1)}, f32[64,256]{1,0:T(8,128)S(1)}, u32[]{:S(2)}, u32[]{:S(2)}) collective-permute-start(f32[64,256]{1,0:T(8,128)S(1)} %get-tuple-element.26), channel_id=1, source_target_pairs={{0,14},{2,0},{4,2},{6,4},{8,6},{10,8},{12,10},{14,12},{1,15},{3,1}... | collective-permute-start | bytes 196616 | tf_op jit(solution)/shard_map/reduce_a/ppermute | solution.py:18
  83.1 5.1 %collective-permute-start.7 = (f32[128,256]{1,0:T(8,128)S(1)}, f32[128,256]{1,0:T(8,128)S(1)}, u32[]{:S(2)}, u32[]{:S(2)}) collective-permute-start(f32[128,256]{1,0:T(8,128)S(1)} %pad_maximum_fusion.8), channel_id=1, source_target_pairs={{0,2},{2,4},{4,6},{6,8},{8,10},{10,12},{12,14},{14,0},{1,3},{3,5},... | collective-permute-start | bytes 393224 | tf_op jit(solution)/shard_map/reduce_a/ppermute | solution.py:18
  83.3 5.3 %collective-permute-start.11 = (f32[128,256]{1,0:T(8,128)S(1)}, f32[128,256]{1,0:T(8,128)S(1)}, u32[]{:S(2)}, u32[]{:S(2)}) collective-permute-start(f32[128,256]{1,0:T(8,128)S(1)} %pad_maximum_fusion.9), channel_id=1, source_target_pairs={{0,14},{2,0},{4,2},{6,4},{8,6},{10,8},{12,10},{14,12},{1,15},{3,1}... | collective-permute-start | bytes 393224 | tf_op jit(solution)/shard_map/reduce_a/ppermute | solution.py:18
  88.3 5.3 %collective-permute-start.8 = (f32[128,256]{1,0:T(8,128)S(1)}, f32[128,256]{1,0:T(8,128)S(1)}, u32[]{:S(2)}, u32[]{:S(2)}) collective-permute-start(f32[128,256]{1,0:T(8,128)S(1)} %bitcast_add_fusion.3), channel_id=1, source_target_pairs={{0,2},{2,4},{4,6},{6,8},{8,10},{10,12},{12,14},{14,0},{1,3},{3,5},... | collective-permute-start | bytes 393224 | tf_op jit(solution)/shard_map/reduce_a/ppermute | solution.py:18
  93.6 5.3 %collective-permute-start.12 = (f32[128,256]{1,0:T(8,128)S(1)}, f32[128,256]{1,0:T(8,128)S(1)}, u32[]{:S(2)}, u32[]{:S(2)}) collective-permute-start(f32[128,256]{1,0:T(8,128)S(1)} %get-tuple-element.21), channel_id=1, source_target_pairs={{0,14},{2,0},{4,2},{6,4},{8,6},{10,8},{12,10},{14,12},{1,15},{3,1}... | collective-permute-start | bytes 393224 | tf_op jit(solution)/shard_map/reduce_a/ppermute | solution.py:18
  93.8 10.8 %collective-permute-start.9 = (f32[128,256]{1,0:T(8,128)S(1)}, f32[128,256]{1,0:T(8,128)S(1)}, u32[]{:S(2)}, u32[]{:S(2)}) collective-permute-start(f32[128,256]{1,0:T(8,128)S(1)} %get-tuple-element.20), channel_id=1, source_target_pairs={{0,2},{2,4},{4,6},{6,8},{8,10},{10,12},{12,14},{14,0},{1,3},{3,5},... | collective-permute-start | bytes 393224 | tf_op jit(solution)/shard_map/reduce_a/ppermute | solution.py:18
  96.1 4.4 %collective-permute-start.17 = (f32[64,256]{1,0:T(8,128)S(1)}, f32[64,256]{1,0:T(8,128)S(1)}, u32[]{:S(2)}, u32[]{:S(2)}) collective-permute-start(f32[64,256]{1,0:T(8,128)S(1)} %get-tuple-element.48), channel_id=1, source_target_pairs={{0,16},{16,32},{32,48},{48,0},{1,17},{17,33},{33,49},{49,1},{2,18}... | collective-permute-start | bytes 196616 | tf_op jit(solution)/shard_map/reduce_b2/ppermute | solution.py:18
  96.2 4.3 %collective-permute-start.19 = (f32[64,256]{1,0:T(8,128)S(1)}, f32[64,256]{1,0:T(8,128)S(1)}, u32[]{:S(2)}, u32[]{:S(2)}) collective-permute-start(f32[64,256]{1,0:T(8,128)S(1)} %get-tuple-element.50), channel_id=1, source_target_pairs={{0,48},{16,0},{32,16},{48,32},{1,49},{17,1},{33,17},{49,33},{2,50}... | collective-permute-start | bytes 196616 | tf_op jit(solution)/shard_map/reduce_b2/ppermute | solution.py:18
  98.9 5.7 %collective-permute-start.13 = (f32[128,256]{1,0:T(8,128)S(1)}, f32[128,256]{1,0:T(8,128)S(1)}, u32[]{:S(2)}, u32[]{:S(2)}) collective-permute-start(f32[128,256]{1,0:T(8,128)S(1)} %bitcast_add_fusion.2), channel_id=1, source_target_pairs={{0,14},{2,0},{4,2},{6,4},{8,6},{10,8},{12,10},{14,12},{1,15},{3,1}... | collective-permute-start | bytes 393224 | tf_op jit(solution)/shard_map/reduce_a/ppermute | solution.py:18
  101.4 7.7 %collective-permute-start.20 = (f32[128,256]{1,0:T(8,128)S(1)}, f32[128,256]{1,0:T(8,128)S(1)}, u32[]{:S(2)}, u32[]{:S(2)}) collective-permute-start(f32[128,256]{1,0:T(8,128)S(1)} %pad_maximum_fusion.11), channel_id=1, source_target_pairs={{0,48},{16,0},{32,16},{48,32},{1,49},{17,1},{33,17},{49,33},{2,50}... | collective-permute-start | bytes 393224 | tf_op jit(solution)/shard_map/reduce_b2/ppermute | solution.py:18
  104.5 5.1 %collective-permute-start.18 = (f32[128,256]{1,0:T(8,128)S(1)}, f32[128,256]{1,0:T(8,128)S(1)}, u32[]{:S(2)}, u32[]{:S(2)}) collective-permute-start(f32[128,256]{1,0:T(8,128)S(1)} %pad_maximum_fusion.10), channel_id=1, source_target_pairs={{0,16},{16,32},{32,48},{48,0},{1,17},{17,33},{33,49},{49,1},{2,18}... | collective-permute-start | bytes 393224 | tf_op jit(solution)/shard_map/reduce_b2/ppermute | solution.py:18
  104.7 9.6 %collective-permute-start.16 = (f32[128,256]{1,0:T(8,128)S(1)}, f32[128,256]{1,0:T(8,128)S(1)}, u32[]{:S(2)}, u32[]{:S(2)}) collective-permute-start(f32[128,256]{1,0:T(8,128)S(1)} %fusion.20), channel_id=1, source_target_pairs={{0,128},{64,192},{128,0},{192,64},{1,129},{65,193},{129,1},{193,65... | collective-permute-start | bytes 393224 | tf_op jit(solution)/shard_map/members/ppermute | solution.py:18
  107.7 7.3 %collective-permute-start.15 = (f32[128,256]{1,0:T(8,128)S(1)}, f32[128,256]{1,0:T(8,128)S(1)}, u32[]{:S(2)}, u32[]{:S(2)}) collective-permute-start(f32[128,256]{1,0:T(8,128)S(1)} %fusion.20), channel_id=1, source_target_pairs={{0,192},{64,0},{128,64},{192,128},{1,193},{65,1},{129,65},{193,129... | collective-permute-start | bytes 393224 | tf_op jit(solution)/shard_map/members/ppermute | solution.py:18
  108.4 6.5 %collective-permute-start.14 = (f32[128,256]{1,0:T(8,128)S(1)}, f32[128,256]{1,0:T(8,128)S(1)}, u32[]{:S(2)}, u32[]{:S(2)}) collective-permute-start(f32[128,256]{1,0:T(8,128)S(1)} %fusion.20), channel_id=1, source_target_pairs={{0,64},{64,128},{128,192},{192,0},{1,65},{65,129},{129,193},{193,1... | collective-permute-start | bytes 393224 | tf_op jit(solution)/shard_map/members/ppermute | solution.py:18
  110.5 6.2 %collective-permute-start.23 = (f32[128,256]{1,0:T(8,128)S(1)}, f32[128,256]{1,0:T(8,128)S(1)}, u32[]{:S(2)}, u32[]{:S(2)}) collective-permute-start(f32[128,256]{1,0:T(8,128)S(1)} %fusion.19), channel_id=1, source_target_pairs={{0,128},{64,192},{128,0},{192,64},{1,129},{65,193},{129,1},{193,65... | collective-permute-start | bytes 393224 | tf_op jit(solution)/shard_map/members/ppermute | solution.py:18
  113.5 5.8 %collective-permute-start.22 = (f32[128,256]{1,0:T(8,128)S(1)}, f32[128,256]{1,0:T(8,128)S(1)}, u32[]{:S(2)}, u32[]{:S(2)}) collective-permute-start(f32[128,256]{1,0:T(8,128)S(1)} %fusion.19), channel_id=1, source_target_pairs={{0,192},{64,0},{128,64},{192,128},{1,193},{65,1},{129,65},{193,129... | collective-permute-start | bytes 393224 | tf_op jit(solution)/shard_map/members/ppermute | solution.py:18
  114.3 5.1 %collective-permute-start.21 = (f32[128,256]{1,0:T(8,128)S(1)}, f32[128,256]{1,0:T(8,128)S(1)}, u32[]{:S(2)}, u32[]{:S(2)}) collective-permute-start(f32[128,256]{1,0:T(8,128)S(1)} %fusion.19), channel_id=1, source_target_pairs={{0,64},{64,128},{128,192},{192,0},{1,65},{65,129},{129,193},{193,1... | collective-permute-start | bytes 393224 | tf_op jit(solution)/shard_map/members/ppermute | solution.py:18
  (8 other events, 202.3 us)
Sparse Core Ops, SparseCore 0:
  27.5 57.0 reduce-scatter.1
